TPU v7x, 32 devices: a whole 2x2x4 slice. The times are simulated.
32 devices in a mesh: front: 4 (over y, core), row: 4 (over z), col: 2 (over x).
Axes of the slice: x: 2, y: 2, z: 4, core: 2. Of those that a mesh axis runs over, the one named last changes fastest.
Arguments:
- pivot_block: bfloat16 [4, 1024, 1024], P('front'), may hold values from -6 to 6
- border: bfloat16 [4, 8192, 1024], P('front', 'row'), may hold values from -6 to 6
- contrib: bfloat16 [4, 8192, 8192], P('front', 'row', 'col'), may hold values from -6 to 6
- inverses: bfloat16 [4, 4, 256, 256], P('front'), may hold values from -0.0625 to 0.0625
- row_tiles: int32 [4, 64], replicated, may hold values from 0 to 79, as said below
- col_tiles: int32 [4, 64], replicated, may hold values from 0 to 79, as said below
- owner: int32 [80], replicated, may hold values from 0 to 79, as said below
- schur_init: bfloat16 [10240, 10240], P(('front', 'row'), 'col'), may hold values from -6 to 6
- block: bfloat16 [10240, 512], P('col'), may hold values from -0.0625 to 0.0625
Outputs:
- schur: float32 [10240, 10240], P(('front', 'row'), 'col')
- product: float32 [10240, 512], P(('front', 'row', 'col'))
Inputs may be any that keep to these rules, and one draw needn't show every extreme that they name: owner is a permutation of 0 .. 79. For each front the 64 entries are distinct. With s = owner[row_tiles[f, i]], each front has exactly 4 entries in each group s // 5; among the 16 entries of one aligned block of a front at most 2 fall in one group, and that many in some block of every draw. For each front the 64 entries are distinct. With s = owner[col_tiles[f, j]], each front has exactly 32 entries in each group s // 40; among the 32 entries of one aligned block of a front at most 32 fall in one group, and that many in some block of every draw.
All inputs are finite; a program needn't handle non-finite values.
Results may differ from a plain program's by a relative error of at most 0.008.
Values may be sent and summed in bfloat16 or wider, within the bound.
No kernel may reach another device: no remote copies, remote signals or barrier semaphores. Data moves between devices by JAX's collectives and lax.ppermute only.
A program may use at most 256 MiB of HBM per device.

v0:
```python
import jax
import jax.numpy as jnp
from jax import lax
from jax.sharding import PartitionSpec as P

TILE = 128


def eliminate(pivot, rows, inverse_set):
    panels = inverse_set.shape[0]
    width = inverse_set.shape[1]
    pivot_now = pivot.astype(jnp.float32)
    rows_now = rows.astype(jnp.float32)
    leaves = []
    for panel_index in range(panels):
        start = panel_index * width
        left = pivot_now[:, start : start + width].astype(jnp.bfloat16)
        below = jnp.arange(pivot.shape[0])[:, None] >= start + width
        lower = jnp.where(
            below, jnp.dot(left, inverse_set[panel_index], preferred_element_type=jnp.float32), 0.0
        ).astype(jnp.bfloat16)
        side = jnp.dot(
            rows_now[:, start : start + width].astype(jnp.bfloat16),
            inverse_set[panel_index],
            preferred_element_type=jnp.float32,
        ).astype(jnp.bfloat16)
        pivot_now = pivot_now - lax.dot_general(
            lower, lower, (((1,), (1,)), ((), ())), preferred_element_type=jnp.float32
        )
        rows_now = rows_now - lax.dot_general(
            side, lower, (((1,), (1,)), ((), ())), preferred_element_type=jnp.float32
        )
        leaves.append(side)
    return jnp.concatenate(leaves, axis=1)


def route_tables(slots, per_group):
    group = slots // per_group
    within = slots % per_group
    count = slots.shape[-1]
    same = group[..., :, None] == group[..., None, :]
    earlier = jnp.arange(count)[None, :] < jnp.arange(count)[:, None]
    rank = jnp.sum((same & earlier).astype(jnp.int32), axis=-1)
    return (group, rank, within)


def pick_sources(group, rank, n_groups, capacity):
    count = group.shape[-1]
    match = (group[None, None, :] == jnp.arange(n_groups)[:, None, None]) & (
        rank[None, None, :] == jnp.arange(capacity)[None, :, None]
    )
    return jnp.sum(match.astype(jnp.int32) * jnp.arange(count)[None, None, :], axis=-1)


def shards(pivot_block, border, contrib, inverses, row_tiles, col_tiles, owner, schur_init, block):
    n_front = lax.axis_size("front")
    n_row = lax.axis_size("row")
    n_col = lax.axis_size("col")
    front_index = lax.axis_index("front")
    row_index = lax.axis_index("row")
    col_index = lax.axis_index("col")
    groups = n_front * n_row
    tiles_all = row_tiles.shape[1]
    slots_all = owner.shape[0]
    row_span = border.shape[1]
    col_span = contrib.shape[2]
    tile_rows = row_span // TILE
    tile_cols = col_span // TILE
    rows_per_group = slots_all // groups
    cols_per_group = slots_all // n_col
    cap_rows = 2 * tiles_all // (n_row * groups)
    cap_cols = 2 * tiles_all // (n_col * n_col)
    share = row_span // n_col
    own_rows = lax.dynamic_slice_in_dim(border[0], col_index * share, share, 0)
    leaves = eliminate(pivot_block[0], own_rows, inverses[0])
    factor = lax.all_gather(leaves, ("row", "col"), axis=0, tiled=True)
    mine = lax.dynamic_slice_in_dim(factor, row_index * row_span, row_span, 0)
    theirs = lax.dynamic_slice_in_dim(factor, col_index * col_span, col_span, 0)
    update = (
        contrib[0].astype(jnp.float32)
        - lax.dot_general(
            mine, theirs, (((1,), (1,)), ((), ())), preferred_element_type=jnp.float32
        )
    ).astype(jnp.bfloat16)
    tiles = update.reshape(tile_rows, TILE, tile_cols, TILE)
    slot_rows = owner[row_tiles].reshape(n_front, n_row, tile_rows)
    slot_cols = owner[col_tiles].reshape(n_front, n_col, tile_cols)
    group_rows, rank_rows, within_rows = route_tables(slot_rows, rows_per_group)
    group_cols, rank_cols, within_cols = route_tables(slot_cols, cols_per_group)
    send_rows = pick_sources(
        group_rows[front_index, row_index], rank_rows[front_index, row_index], groups, cap_rows
    )
    my_group = front_index * n_row + row_index
    flat_group = group_rows.reshape(groups, tile_rows)
    flat_rank = rank_rows.reshape(groups, tile_rows)
    flat_within = within_rows.reshape(groups, tile_rows)
    hit_rows = (flat_group == my_group)[:, None, :] & (
        flat_rank[:, None, :] == jnp.arange(cap_rows)[None, :, None]
    )
    place_rows = jnp.sum(
        (
            hit_rows[None]
            & (flat_within[None, :, None, :] == jnp.arange(rows_per_group)[:, None, None, None])
        ).astype(jnp.int32),
        axis=-1,
    ).astype(jnp.bfloat16)
    hit_cols = (group_cols == col_index)[:, :, None, :] & (
        rank_cols[:, :, None, :] == jnp.arange(cap_cols)[None, None, :, None]
    )
    place_cols = jnp.sum(
        (
            hit_cols[None]
            & (
                within_cols[None, :, :, None, :]
                == jnp.arange(cols_per_group)[:, None, None, None, None]
            )
        ).astype(jnp.int32),
        axis=-1,
    ).astype(jnp.bfloat16)
    place_cols = jnp.repeat(place_cols, n_row, axis=1)
    send_cols = pick_sources(
        group_cols[front_index, col_index], rank_cols[front_index, col_index], n_col, cap_cols
    )
    by_rows = jnp.take(tiles, send_rows.reshape(-1), axis=0)
    by_both = jnp.take(by_rows, send_cols.reshape(-1), axis=2)
    outgoing = by_both.reshape(groups, cap_rows, TILE, n_col, cap_cols, TILE).transpose(
        0, 3, 1, 4, 2, 5
    )
    outgoing = outgoing.reshape(groups * n_col, cap_rows, cap_cols, TILE, TILE)
    received = lax.all_to_all(
        outgoing, ("front", "row", "col"), split_axis=0, concat_axis=0, tiled=True
    )
    received = received.reshape(groups, n_col, cap_rows, cap_cols, TILE, TILE)
    gathered = jnp.einsum(
        "bgcm,gckmxy->bgkxy", place_cols, received, preferred_element_type=jnp.float32
    ).astype(jnp.bfloat16)
    summed = jnp.einsum("agk,bgkxy->abxy", place_rows, gathered, preferred_element_type=jnp.float32)
    schur = schur_init.astype(jnp.float32) + summed.transpose(0, 2, 1, 3).reshape(
        rows_per_group * TILE, cols_per_group * TILE
    )
    rounded = schur.astype(jnp.bfloat16)
    product = lax.psum_scatter(
        jnp.dot(rounded, block, preferred_element_type=jnp.float32),
        "col",
        scatter_dimension=0,
        tiled=True,
    )
    return (schur, product)


def solution(mesh):
    in_specs = (
        P("front", None, None),
        P("front", "row", None),
        P("front", "row", "col"),
        P("front", None, None, None),
        P(),
        P(),
        P(),
        P(("front", "row"), "col"),
        P("col", None),
    )
    out_specs = (P(("front", "row"), "col"), P(("front", "row", "col"), None))
    return jax.shard_map(shards, mesh=mesh, in_specs=in_specs, out_specs=out_specs, check_vma=False)
```

profile of v0, /device:TPU:0, one launch (start us, length us, event | category | flops | bytes accessed | tf_op | source)
XLA Modules:
  0.0 2108.5 jit_solution(10007459200147742277)
XLA Ops:
  7.3 1.9 dynamic-slice_bitcast_fusion
  13.5 2.8 fusion.59
  17.1 2.0 copy-done.4
  19.4 4.5 fusion.21
  23.9 1.9 convolution_convert_fusion
  27.5 2.2 gather_fusion
  36.6 221.0 %all-gather.2.cloned.1.call-done = bf16[8192,1024]{0,1:T(8,128)(2,1)} async-done(((bf16[1024,1024]{0,1:T(8,128)(2,1)}), bf16[8192,1024]{0,1:T(8,128)(2,1)}) %all-gather.2.cloned.1.call-update) | async-done | bytes 16777232 | tf_op jit(solution)/shard_map/all_gather | solution.py:76
  257.6 25.7 %fusion.12 = bf16[256,8,32,128]{3,1,2,0:T(8,128)(2,1)} fusion(bf16[8192,1024]{0,1:T(8,128)(2,1)} %all-gather.2.cloned.1.call-done, s32[]{:T(128)S(6)} %select_n.154, bf16[1,2048,4096]{2,1,0:T(8,128)(2,1)} %param.11, s32[]{:T(128)S(6)} %select_n.153), kind=kOutput, calls=%fused_computation.17 | convolution fusion | flops 17205035008 | bytes 46137352 | tf_op jit(solution)/shard_map/dot_general | solution.py:81
  283.3 15.1 copy.36
  298.3 18.7 gather_fusion.2
  317.1 22.8 %broadcast_select_fusion = bf16[32,128,32,128]{3,2,1,0:T(8,128)(2,1)} fusion(bf16[32,128,32,128]{3,2,1,0:T(8,128)(2,1)} %gather_fusion.2, pred[32]{0:T(512)(128)(4,1)S(1)} %compare_and_fusion.1), kind=kLoop, calls=%fused_computation.13 | loop fusion | flops 16777216 | bytes 67108896 | tf_op jit(solution)/shard_map/jit(_take)/select_n | solution.py:124
  339.9 23.4 %copy.24 = bf16[32,128,32,128]{3,1,0,2:T(8,128)(2,1)} copy(bf16[32,128,32,128]{3,2,1,0:T(8,128)(2,1)} %broadcast_select_fusion) | data formatting | bytes 67108864 | tf_op jit(solution)/shard_map/jit(_take)/select_n | solution.py:124
  363.3 35.9 %gather_fusion.3 = bf16[64,32,128,128]{3,2,1,0:T(8,128)(2,1)} fusion(bf16[32,128,32,128]{3,1,0,2:T(8,128)(2,1)} %copy.24, s32[1024]{0:T(1024)S(1)} %pad_clamp_fusion), kind=kCustom, calls=%fused_computation.3 | custom fusion | bytes 134217984 | tf_op jit(solution)/shard_map/jit(_take)/gather | solution.py:125
  399.2 44.4 %copy_select_fusion = bf16[16,2,128,2,32,128]{5,2,4,1,3,0:T(8,128)(2,1)} fusion(bf16[16,2,128,2,32,128]{5,2,1,0,4,3:T(8,128)(2,1)} %bitcast.16, pred[2,32]{1,0:T(4,128)(4,1)S(1)} %compare_and_fusion.2), kind=kLoop, calls=%fused_computation.7 | loop fusion | flops 33554432 | bytes 134217792 | tf_op jit(solution)/shard_map/jit(_take)/select_n | solution.py:125
  443.7 5.1 all-to-all-start
  449.1 2.0 convert_reduce_fusion
  451.6 1442.9 %all-to-all-done = bf16[32,2,32,128,128]{4,3,2,1,0:T(8,128)(2,1)} async-done(((bf16[32,2,32,128,128]{4,3,2,1,0:T(8,128)(2,1)}), bf16[32,2,32,128,128]{4,3,2,1,0:T(8,128)(2,1)}, u32[]{:S(2)}, u32[]{:S(2)}) %all-to-all-start) | async-done | bytes 67108896 | tf_op jit(solution)/shard_map/all_to_all | solution.py:130
  1894.6 66.8 %fusion.2 = bf16[40,16,2,128,128]{4,0,3,2,1:T(8,128)(2,1)} fusion(bf16[40,16,2,32,1,1]{0,3,2,5,4,1:T(8,128)(2,1)S(1)} %bitcast.89, bf16[16,2,2,32,128,128]{5,4,3,2,1,0:T(8,128)(2,1)} %bitcast.19), kind=kOutput, calls=%fused_computation.8 | convolution fusion | flops 2705326080 | bytes 109133824 | tf_op jit(solution)/shard_map/bgcm,gckmxy->bgkxy/dot_general | solution.py:134
  1961.4 34.2 %fusion.8 = f32[5,128,40,128]{3,0,1,2:T(8,128)} fusion(bf16[40,16,2,128,128]{4,0,3,2,1:T(8,128)(2,1)} %fusion.2, bf16[5,16,2,1,1]{1,2,0,4,3:T(2,128)(2,1)S(1)} %convert_bitcast_fusion), kind=kOutput, calls=%fused_computation.15 | convolution fusion | flops 209715200 | bytes 55050560 | tf_op jit(solution)/shard_map/agk,bgkxy->abxy/dot_general | solution.py:137
  1995.6 9.8 copy.29
  2005.4 6.0 bitcast_add_fusion
  2011.4 4.9 copy-done.2
  2016.4 4.6 fusion.15
  2021.0 80.4 %reduce-scatter.2.cloned.1.call-done = f32[320,512]{1,0:T(8,128)} async-done(((f32[640,512]{1,0:T(8,128)}), f32[320,512]{1,0:T(8,128)}) %reduce-scatter.2.cloned.1.call-update) | async-done | bytes 655376 | tf_op jit(solution)/shard_map/reduce_scatter | solution.py:142
  (114 shorter events, 14.6 us)
Async XLA Ops:
  7.2 20.4 copy-start
  7.2 3.3 copy-start.6
  7.2 3.3 copy-start.5
  7.2 250.4 %all-gather.2.cloned.1.call-start = ((), (), s32[]{:S(2)}) async-start(), calls=%async_computation.2 | async-start | bytes 18874368 | tf_op jit(solution)/shard_map/all_gather | solution.py:76
  11.6 2.0 copy-start.3
  17.1 2.0 copy-start.4
  23.9 3.5 copy-start.18
  23.9 3.5 copy-start.19
  30.3 253.0 %copy-start.13 = (s32[256]{0:T(256)}, s32[256]{0:T(256)S(1)}, u32[]{:S(2)}) copy-start(s32[256]{0:T(256)S(1)} %get-tuple-element.7) | copy-start | bytes 3076
  31.5 0.6 copy-start.9
  34.5 248.7 %copy-start.7 = (s32[4,2,32]{2,1,0:T(2,128)}, s32[4,2,32]{2,1,0:T(2,128)S(1)}, u32[]{:S(2)}) copy-start(s32[4,2,32]{2,1,0:T(2,128)S(1)} %rem.73) | copy-start | bytes 3076
  443.6 5.2 copy-start.14
  443.6 5.3 copy-start.8
  443.6 5.4 copy-start.12
  443.6 5.4 copy-start.15
  443.6 7.5 copy-start.16
  443.6 7.6 copy-start.17
  443.6 7.7 copy-start.10
  443.7 1450.9 %all-to-all-start = ((bf16[32,2,32,128,128]{4,3,2,1,0:T(8,128)(2,1)}), bf16[32,2,32,128,128]{4,3,2,1,0:T(8,128)(2,1)}, u32[]{:S(2)}, u32[]{:S(2)}) async-start(bf16[32,2,32,128,128]{4,3,2,1,0:T(8,128)(2,1)} %bitcast.18), calls=%async_computation | async-start | bytes 134217728 | tf_op jit(solution)/shard_map/all_to_all | solution.py:130
  448.8 1652.7 %reduce-scatter.2.cloned.1.call-start = ((), (), s32[]{:S(2)}) async-start(), calls=%async_computation.3 | async-start | bytes 1966080 | tf_op jit(solution)/shard_map/reduce_scatter | solution.py:142
  1961.4 55.0 %slice-start = ((s8[5242880]{0:T(1024)(128)(4,1)}), s8[1048576]{0:T(1024)(128)(4,1)S(1)}, s32[]{:S(2)}) async-start(s8[5242880]{0:T(1024)(128)(4,1)} %bitcast.91), calls=%async_computation.4 | async-start | bytes 2097152
  1995.6 20.7 slice-start.1
  2011.4 5.0 copy-start.2
  2016.4 85.1 %copy-start.1 = (s32[80]{0:T(128)S(1)}, s32[80]{0:T(128)}, u32[]{:S(2)}) copy-start(s32[80]{0:T(128)} %param.15) | copy-start | bytes 964
  (1 other events, 0.6 us)
Sparse Core Ops, SparseCore 0:
  27.5 230.0 all-gather.1
  2021.1 80.2 reduce-scatter.1
where the time goes:
time: 2110 us
  waiting for transfers between devices  1740 us (82%)
  matrix products  145 us (7%)
  local copies, waits for them, and re-layouts  119 us (6%)
  other arithmetic  80 us (4%)
    all_to_all x1, waiting for transfers between devices, shards(): lax.all_to_all(outgoing, ('front', 'row', 'col'), split_axis=0, concat_ax...  1440 us
    all_gather x1, waiting for transfers between devices, shards(): factor = lax.all_gather(leaves, ('row', 'col'), axis=0, tiled=True)  221 us
    reduce_scatter x1, waiting for transfers between devices, shards(): lax.psum_scatter(jnp.dot(rounded, block, preferred_element_type=jnp.float...  80.4 us
    dot_general x1, matrix products, shards(): jnp.einsum('bgcm,gckmxy->bgkxy', place_cols, received, preferred_element_...  66.8 us
    select_n x2, other arithmetic, shards(): by_both = jnp.take(by_rows, send_cols.reshape(-1), axis=2)  44.4 us
  transfers between devices with their start and end apart: 3, of which 3 were waited for; matrix products, arithmetic and copies ran while one was open for 0% of the time, Pallas kernels for 0%

commit v1 on v0

--- a/solution.py
+++ b/solution.py
@@ -4,6 +4,24 @@
 from jax.sharding import PartitionSpec as P
 
 TILE = 128
+
+
+def in_order(blocks, dim):
+    dims = list(blocks.shape[1:])
+    dims[dim] *= blocks.shape[0]
+    return jnp.moveaxis(blocks, 0, dim).reshape(dims)
+
+
+def collected_by_bits(shard, axis):
+    size = lax.axis_size(axis)
+    blocks = shard[None]
+    for level in range(size.bit_length() - 1):
+        distance = 1 << level
+        other = lax.ppermute(blocks, axis, [(i, i ^ distance) for i in range(size)])
+        both = jnp.stack([blocks, other])
+        upper = lax.axis_index(axis) >> level & 1
+        blocks = jnp.where(upper == 0, both, both[::-1]).reshape(-1, *shard.shape)
+    return blocks
 
 
 def eliminate(pivot, rows, inverse_set):
@@ -73,7 +91,7 @@
     share = row_span // n_col
     own_rows = lax.dynamic_slice_in_dim(border[0], col_index * share, share, 0)
     leaves = eliminate(pivot_block[0], own_rows, inverses[0])
-    factor = lax.all_gather(leaves, ("row", "col"), axis=0, tiled=True)
+    factor = in_order(collected_by_bits(leaves, ("row", "col")), 0)
     mine = lax.dynamic_slice_in_dim(factor, row_index * row_span, row_span, 0)
     theirs = lax.dynamic_slice_in_dim(factor, col_index * col_span, col_span, 0)
     update = (

time: 2110 us -> 2450 us (1.16)
  waiting for transfers between devices: 1740 us -> 2000 us
  other arithmetic: 80 us -> 131 us
    ppermute x0 -> x3, waiting for transfers between devices: none -> 475 us  [collected_by_bits(): other = lax.ppermute(blocks, axis, [(i, i ^ distance) for i in range(size)])]
    all_gather x1 -> x0, waiting for transfers between devices: 221 us -> none  [shards(): factor = lax.all_gather(leaves, ('row', 'col'), axis=0, tiled=True)]
    another operation x0 -> x5, other arithmetic: none -> 27.9 us  [collected_by_bits(): both = jnp.stack([blocks, other])]
  transfers between devices with their start and end apart: 3 -> 5, of which waited for: 3 -> 5; matrix products, arithmetic and copies ran while one was open for 0% -> 1% of each run, Pallas kernels for 0% -> 0%
where the time goes in v1:
time: 2450 us; the launch traced here: 2440 us
  waiting for transfers between devices  2000 us (82%)
  matrix products  147 us (6%)
  local copies, waits for them, and re-layouts  141 us (6%)
  other arithmetic  131 us (5%)
    all_to_all x1, waiting for transfers between devices, shards(): lax.all_to_all(outgoing, ('front', 'row', 'col'), split_axis=0, concat_ax...  1440 us
    ppermute x3, waiting for transfers between devices, collected_by_bits(): other = lax.ppermute(blocks, axis, [(i, i ^ distance) for i in range(size)])  475 us
    reduce_scatter x1, waiting for transfers between devices, shards(): lax.psum_scatter(jnp.dot(rounded, block, preferred_element_type=jnp.float...  80.4 us
    dot_general x1, matrix products, shards(): jnp.einsum('bgcm,gckmxy->bgkxy', place_cols, received, preferred_element_...  66.8 us
  transfers between devices with their start and end apart: 5, of which 5 were waited for; matrix products, arithmetic and copies ran while one was open for 1% of the time, Pallas kernels for 0%

profile of v1, /device:TPU:0, one launch (start us, length us, event | category | flops | bytes accessed | tf_op | source)
XLA Modules:
  0.0 2444.3 jit_solution(13789329169824528850)
XLA Ops:
  26.6 5.3 fusion.34
  34.8 45.9 %collective-permute-done = bf16[1,1024,1024]{1,2,0:T(8,128)(2,1)} collective-permute-done((bf16[1,1024,1024]{1,2,0:T(8,128)(2,1)}, bf16[1,1024,1024]{1,2,0:T(8,128)(2,1)}, u32[]{:S(2)}, u32[]{:S(2)}) %collective-permute-start) | collective-permute-done | bytes 2097184 | tf_op jit(solution)/shard_map/ppermute | solution.py:20
  89.6 90.2 %collective-permute-done.1 = bf16[2,1024,1024]{1,2,0:T(8,128)(2,1)} collective-permute-done((bf16[2,1024,1024]{1,2,0:T(8,128)(2,1)}, bf16[2,1024,1024]{1,2,0:T(8,128)(2,1)}, u32[]{:S(2)}, u32[]{:S(2)}) %collective-permute-start.1) | collective-permute-done | bytes 4194336 | tf_op jit(solution)/shard_map/ppermute | solution.py:20
  179.8 7.6 pad_maximum_fusion.1
  187.5 13.5 reverse_select_fusion.1
  200.9 11.4 copy.29
  224.1 11.4 copy.30
  235.5 338.5 %collective-permute-done.2 = bf16[4,1024,1024]{2,1,0:T(8,128)(2,1)} collective-permute-done((bf16[4,1024,1024]{2,1,0:T(8,128)(2,1)}, bf16[4,1024,1024]{2,1,0:T(8,128)(2,1)}, u32[]{:S(2)}, u32[]{:S(2)}) %collective-permute-start.2) | collective-permute-done | bytes 8388640 | tf_op jit(solution)/shard_map/ppermute | solution.py:20
  574.1 8.0 pad_maximum_fusion
  582.1 10.6 reverse_select_fusion
  592.7 26.4 %fusion.12 = bf16[256,8,32,128]{3,1,2,0:T(8,128)(2,1)} fusion(bf16[8192,1024]{1,0:T(8,128)(2,1)} %bitcast.104, s32[]{:T(128)S(6)} %select_n.184, bf16[1,2048,4096]{2,1,0:T(8,128)(2,1)} %param.11, s32[]{:T(128)S(6)} %select_n.183), kind=kOutput, calls=%fused_computation.21 | convolution fusion | flops 17205035008 | bytes 46137352 | tf_op jit(solution)/shard_map/dot_general | solution.py:99
  619.1 15.1 copy.44
  634.1 18.7 gather_fusion.2
  652.9 22.8 broadcast_select_fusion
  675.7 23.4 copy.32
  699.0 35.9 %gather_fusion.3 = bf16[64,32,128,128]{3,2,1,0:T(8,128)(2,1)} fusion(bf16[32,128,32,128]{3,1,0,2:T(8,128)(2,1)} %copy.32, s32[1024]{0:T(1024)S(1)} %pad_clamp_fusion), kind=kCustom, calls=%fused_computation.3 | custom fusion | bytes 134217984 | tf_op jit(solution)/shard_map/jit(_take)/gather | solution.py:143
  734.9 44.2 %copy_select_fusion = bf16[16,2,128,2,32,128]{5,2,4,1,3,0:T(8,128)(2,1)} fusion(bf16[16,2,128,2,32,128]{5,2,1,0,4,3:T(8,128)(2,1)} %bitcast.26, pred[2,32]{1,0:T(4,128)(4,1)S(1)} %copy-done.22), kind=kLoop, calls=%fused_computation.7 | loop fusion | flops 33554432 | bytes 134217792 | tf_op jit(solution)/shard_map/jit(_take)/select_n | solution.py:143
  779.2 5.1 all-to-all-start
  786.9 1443.2 %all-to-all-done = bf16[32,2,32,128,128]{4,3,2,1,0:T(8,128)(2,1)} async-done(((bf16[32,2,32,128,128]{4,3,2,1,0:T(8,128)(2,1)}), bf16[32,2,32,128,128]{4,3,2,1,0:T(8,128)(2,1)}, u32[]{:S(2)}, u32[]{:S(2)}) %all-to-all-start) | async-done | bytes 67108896 | tf_op jit(solution)/shard_map/all_to_all | solution.py:148
  2230.1 66.8 %fusion.2 = bf16[40,16,2,128,128]{4,0,3,2,1:T(8,128)(2,1)} fusion(bf16[40,16,2,32,1,1]{0,3,2,5,4,1:T(8,128)(2,1)S(1)} %bitcast.106, bf16[16,2,2,32,128,128]{5,4,3,2,1,0:T(8,128)(2,1)} %bitcast.29), kind=kOutput, calls=%fused_computation.8 | convolution fusion | flops 2705326080 | bytes 109133824 | tf_op jit(solution)/shard_map/bgcm,gckmxy->bgkxy/dot_general | solution.py:152
  2297.0 34.3 %fusion.8 = f32[5,128,40,128]{3,0,1,2:T(8,128)} fusion(bf16[40,16,2,128,128]{4,0,3,2,1:T(8,128)(2,1)} %fusion.2, bf16[5,16,2,1,1]{1,2,0,4,3:T(2,128)(2,1)S(1)} %convert_bitcast_fusion), kind=kOutput, calls=%fused_computation.18 | convolution fusion | flops 209715200 | bytes 55050560 | tf_op jit(solution)/shard_map/agk,bgkxy->abxy/dot_general | solution.py:155
  2331.3 9.8 copy.37
  2341.1 6.0 bitcast_add_fusion
  2356.7 80.4 %reduce-scatter.2.cloned.1.call-done = f32[320,512]{1,0:T(8,128)} async-done(((f32[640,512]{1,0:T(8,128)}), f32[320,512]{1,0:T(8,128)}) %reduce-scatter.2.cloned.1.call-update) | async-done | bytes 655376 | tf_op jit(solution)/shard_map/reduce_scatter | solution.py:160
  (131 shorter events, 54.8 us)
Async XLA Ops:
  7.2 207.8 %copy-start = (s32[80]{0:T(128)S(1)}, s32[80]{0:T(128)}, u32[]{:S(2)}) copy-start(s32[80]{0:T(128)} %param.15) | copy-start | bytes 964
  7.2 4.6 copy-start.6
  19.9 4.7 copy-start.5
  31.8 48.9 %collective-permute-start = (bf16[1,1024,1024]{1,2,0:T(8,128)(2,1)}, bf16[1,1024,1024]{1,2,0:T(8,128)(2,1)}, u32[]{:S(2)}, u32[]{:S(2)}) collective-permute-start(bf16[1,1024,1024]{1,2,0:T(8,128)(2,1)} %get-tuple-element.9), channel_id=1, source_target_pairs={{0,1},{1,0},{2,3},{3,2},{4,5},{5,4},{6,7},{7,6},{8,9},{9,8},{10,11... | collective-permute-start | bytes 6291464 | tf_op jit(solution)/shard_map/ppermute | solution.py:20
  87.8 92.1 %collective-permute-start.1 = (bf16[2,1024,1024]{1,2,0:T(8,128)(2,1)}, bf16[2,1024,1024]{1,2,0:T(8,128)(2,1)}, u32[]{:S(2)}, u32[]{:S(2)}) collective-permute-start(bf16[2,1024,1024]{1,2,0:T(8,128)(2,1)} %get-tuple-element.7), channel_id=1, source_target_pairs={{0,2},{1,3},{2,0},{3,1},{4,6},{5,7},{6,4},{7,5},{8,10},{9,11},{10,... | collective-permute-start | bytes 12582920 | tf_op jit(solution)/shard_map/ppermute | solution.py:20
  200.9 13.9 copy-start.20
  200.9 13.9 copy-start.21
  212.3 361.7 %collective-permute-start.2 = (bf16[4,1024,1024]{2,1,0:T(8,128)(2,1)}, bf16[4,1024,1024]{2,1,0:T(8,128)(2,1)}, u32[]{:S(2)}, u32[]{:S(2)}) collective-permute-start(bf16[4,1024,1024]{2,1,0:T(8,128)(2,1)} %copy.29), channel_id=1, source_target_pairs={{0,4},{1,5},{2,6},{3,7},{4,0},{5,1},{6,2},{7,3},{8,12},{9,13},{10,... | collective-permute-start | bytes 25165832 | tf_op jit(solution)/shard_map/ppermute | solution.py:20
  217.4 18.1 copy-start.15
  221.6 13.9 copy-start.9
  699.0 35.9 %copy-start.22 = (pred[2,32]{1,0:T(4,128)(4,1)S(1)}, pred[2,32]{1,0:T(4,128)(4,1)}, u32[]{:S(2)}) copy-start(pred[2,32]{1,0:T(4,128)(4,1)} %compare_and_fusion.2) | copy-start | bytes 196
  779.2 5.2 copy-start.16
  779.2 5.3 copy-start.10
  779.2 5.4 copy-start.14
  779.2 5.4 copy-start.17
  779.2 7.2 copy-start.18
  779.2 7.2 copy-start.19
  779.2 7.3 copy-start.12
  779.2 1450.9 %all-to-all-start = ((bf16[32,2,32,128,128]{4,3,2,1,0:T(8,128)(2,1)}), bf16[32,2,32,128,128]{4,3,2,1,0:T(8,128)(2,1)}, u32[]{:S(2)}, u32[]{:S(2)}) async-start(bf16[32,2,32,128,128]{4,3,2,1,0:T(8,128)(2,1)} %bitcast.28), calls=%async_computation | async-start | bytes 134217728 | tf_op jit(solution)/shard_map/all_to_all | solution.py:148
  784.3 1652.9 %reduce-scatter.2.cloned.1.call-start = ((), (), s32[]{:S(2)}) async-start(), calls=%async_computation.2 | async-start | bytes 1966080 | tf_op jit(solution)/shard_map/reduce_scatter | solution.py:160
  2297.0 55.1 %slice-start = ((s8[5242880]{0:T(1024)(128)(4,1)}), s8[1048576]{0:T(1024)(128)(4,1)S(1)}, s32[]{:S(2)}) async-start(s8[5242880]{0:T(1024)(128)(4,1)} %bitcast.108), calls=%async_computation.3 | async-start | bytes 2097152
  2331.3 20.8 slice-start.1
  2347.1 5.0 copy-start.2
  2352.1 85.1 %copy-start.1 = (s32[80]{0:T(128)S(1)}, s32[80]{0:T(128)}, u32[]{:S(2)}) copy-start(s32[80]{0:T(128)} %param.15) | copy-start | bytes 964
  (6 other events, 12.1 us)
Sparse Core Ops, SparseCore 0:
  2356.9 80.2 reduce-scatter.1
